TPU v7x, 256 devices: a whole 4x4x8 slice. The times are simulated.
256 devices in a mesh: dp: 4 (over x_hi, core), ctx: 64 (over y, z, x_lo).
Axes of the slice: x: 4 (x_hi: 2, x_lo: 2; x = x_hi * 2 + x_lo), y: 4, z: 8, core: 2. Of those that a mesh axis runs over, the one named last changes fastest.
Arguments:
- frames: bfloat16 [4, 12288, 1024], P('dp', 'ctx'), may hold values from -60 to 60
- lengths: int32 [4], P('dp'), may hold values from 6144 to 12288, as said below
- w_qkv: bfloat16 [1024, 1536], replicated, may hold values from -0.9 to 0.9
- w_out: bfloat16 [512, 1024], replicated, may hold values from -0.25 to 0.25
- w_pw1: bfloat16 [1024, 2048], replicated, may hold values from -0.1875 to 0.1875
- conv_taps: float32 [31, 1024], replicated, may hold values from -1 to 1
- w_pw2: bfloat16 [1024, 1024], replicated, may hold values from -0.1875 to 0.1875
Outputs:
- encoded: bfloat16 [4, 12288, 1024], P('dp', 'ctx')
Inputs may be any that keep to these rules, and one draw needn't show every extreme that they name: `lengths`: the valid frames of a recording are its first ones; some recording has all 12288 frames valid.
All inputs are finite; a program needn't handle non-finite values.
Results may differ from a plain program's by a relative error of at most 0.011.
Values may be sent and summed in bfloat16 or wider, within the bound.
A program may use at most 256 MiB of HBM per device.

v0:
```python
import jax
import jax.numpy as jnp
from jax import lax
from jax.sharding import PartitionSpec as P

HEADS = 8
epsilon = 1e-05
masked_score = -1e30


def padded_2(cells, sides, width):
    for axis, dim in sides:
        count = lax.axis_size(axis)
        ends = count - 1
        head = lax.slice_in_dim(cells, 0, width, axis=dim)
        tail = lax.slice_in_dim(cells, cells.shape[dim] - width, cells.shape[dim], axis=dim)
        cells = jnp.concatenate(
            [
                lax.ppermute(tail, axis, [(i, (i + 1) % count) for i in range(ends)]),
                cells,
                lax.ppermute(head, axis, [((i + 1) % count, i) for i in range(ends)]),
            ],
            axis=dim,
        )
    return cells


def to_bf16(value):
    return lax.optimization_barrier(value.astype(jnp.bfloat16))


def layer_norm(value):
    center = value - jnp.mean(value, axis=-1, keepdims=True)
    spread = jnp.mean(center * center, axis=-1, keepdims=True)
    return center * lax.rsqrt(spread + epsilon)


def depthwise(padded, conv_taps, count):
    total = jnp.zeros((count, padded.shape[1]), jnp.float32)
    for tap_index in range(conv_taps.shape[0]):
        total = total + conv_taps[tap_index] * padded[tap_index : tap_index + count].astype(
            jnp.float32
        )
    return total


def gate_rows(stream_rows, spots, limit, w_pw1):
    gated = jnp.dot(
        to_bf16(layer_norm(stream_rows.astype(jnp.float32))),
        w_pw1,
        preferred_element_type=jnp.float32,
    )
    half_cols = gated.shape[1] // 2
    result = gated[:, :half_cols] * jax.nn.sigmoid(gated[:, half_cols:])
    return to_bf16(jnp.where((spots < limit)[:, None], result, 0.0))


def attend_block(carry, query_heads, key_piece, value_piece, limit):
    run_max, run_sum, run_acc = carry
    count = key_piece.shape[0]
    head_count = query_heads.shape[1]
    head_size = query_heads.shape[2]
    key_heads = key_piece.reshape(count, head_count, head_size)
    value_heads = value_piece.reshape(count, head_count, head_size)
    scores = jnp.einsum("qhd,khd->hqk", query_heads, key_heads, preferred_element_type=jnp.float32)
    live = jnp.arange(count, dtype=jnp.int32) < limit
    masked = jnp.where(live, scores, masked_score)
    new_max = jnp.maximum(run_max, jnp.max(masked, axis=-1))
    weights = jnp.where(live, jnp.exp(masked - new_max[:, :, None]), 0.0)
    scale_old = jnp.exp(run_max - new_max)
    new_sum = jnp.sum(weights, axis=-1)
    product = jnp.einsum(
        "hqk,khd->qhd", to_bf16(weights), value_heads, preferred_element_type=jnp.float32
    )
    new_acc = run_acc * scale_old.T[:, :, None] + product
    return (new_max, new_sum, new_acc)


def per_device(frames, lengths, w_qkv, w_out, w_pw1, conv_taps, w_pw2):
    stream = frames[0]
    frame_rows = stream.shape[0]
    my_index = lax.axis_index("ctx")
    my_start = my_index * frame_rows
    limit = lengths[0]
    positions = my_start + jnp.arange(frame_rows, dtype=jnp.int32)
    valid = positions < limit
    normed = to_bf16(layer_norm(stream.astype(jnp.float32)))
    projected = jnp.dot(normed, w_qkv, preferred_element_type=jnp.float32)
    inner = w_out.shape[0]
    head_size = inner // HEADS
    queries = to_bf16(projected[:, :inner] * head_size ** (-0.5)).reshape(
        frame_rows, HEADS, head_size
    )
    keys = to_bf16(projected[:, inner : 2 * inner])
    values = to_bf16(projected[:, 2 * inner :])
    initial = (
        jnp.full((HEADS, frame_rows), masked_score, jnp.float32),
        jnp.zeros((HEADS, frame_rows), jnp.float32),
        jnp.zeros((frame_rows, HEADS, head_size), jnp.float32),
    )
    run_max, run_sum, run_acc = attend_block(
        initial,
        queries,
        lax.all_gather(keys, "ctx", axis=0, tiled=True),
        lax.all_gather(values, "ctx", axis=0, tiled=True),
        limit,
    )
    attended = to_bf16(run_acc / run_sum.T[:, :, None]).reshape(frame_rows, inner)
    first = to_bf16(
        stream.astype(jnp.float32) + jnp.dot(attended, w_out, preferred_element_type=jnp.float32)
    )
    half_width = conv_taps.shape[0] // 2
    gated_own = gate_rows(first, positions, limit, w_pw1)
    padded = padded_2(gated_own, (("ctx", 0),), half_width)
    conv = depthwise(padded, conv_taps, frame_rows)
    swished = to_bf16(jax.nn.silu(layer_norm(conv)))
    second = first.astype(jnp.float32) + jnp.dot(swished, w_pw2, preferred_element_type=jnp.float32)
    encoded = jnp.where(valid[:, None], layer_norm(second), 0.0).astype(jnp.bfloat16)
    return encoded[None]


def solution(mesh):
    in_specs = (P("dp", "ctx", None), P("dp"), P(), P(), P(), P(), P())
    out_specs = P("dp", "ctx", None)
    return jax.shard_map(
        per_device, mesh=mesh, in_specs=in_specs, out_specs=out_specs, check_vma=False
    )
```

profile of v0, /device:TPU:2, one launch (start us, length us, event | category | flops | bytes accessed | tf_op | source)
XLA Modules:
  0.0 736.1 jit_solution(17029172689337861144)
XLA Ops:
  6.5 1.3 convert_reduce_fusion.1
  7.8 1.2 fusion.13
  9.1 1.2 fusion.14
  10.3 1.9 fusion.56
  12.2 0.8 fusion.52
  13.0 0.7 all-gather.5.cloned.1.call-update
  13.7 1.0 fusion.50
  16.1 1.8 fusion.54
  18.0 322.8 %all-gather.3.cloned.1.call-done = bf16[12288,512]{1,0:T(8,128)(2,1)} async-done(((bf16[192,512]{1,0:T(8,128)(2,1)}), bf16[12288,512]{1,0:T(8,128)(2,1)}) %all-gather.3.cloned.1.call-update) | async-done | bytes 12582928 | tf_op jit(solution)/shard_map/all_gather | solution.py:104
  340.7 16.6 %copy.12 = bf16[12288,512]{0,1:T(8,128)(2,1)} copy(bf16[12288,512]{1,0:T(8,128)(2,1)} %all-gather.3.cloned.1.call-done) | data formatting | bytes 25165824 | tf_op jit(solution)/shard_map/all_gather | solution.py:104
  357.3 31.0 %select_reduce_fusion = (f32[8,192]{1,0:T(8,128)S(1)}, f32[8,192,12288]{2,1,0:T(8,128)}) fusion(pred[12288]{0:T(1024)(128)(4,1)S(1)} %iota_compare_fusion, bf16[192,8,64]{0,2,1:T(8,128)(2,1)S(1)} %bitcast.79, bf16[12288,8,64]{0,2,1:T(8,128)(2,1)} %bitcast.78), kind=kOutput, calls=%fused_computation.1 | convolution fusion | flops 2453666304 | bytes 88295424 | tf_op jit(solution)/shard_map/qhd,khd->hqk/dot_general | solution.py:65
  388.4 37.7 %fusion = (f32[8,192]{1,0:T(8,128)S(1)}, bf16[8,192,12288]{2,1,0:T(8,128)(2,1)}) fusion(f32[8,192,12288]{2,1,0:T(8,128)} %get-tuple-element.49, f32[8,192]{1,0:T(8,128)S(1)} %get-tuple-element.45, pred[12288]{0:T(1024)(128)(4,1)S(1)} %iota_compare_fusion), kind=kLoop, calls=%fused_computation.2 | loop fusion | flops 94370304 | bytes 113270784 | tf_op jit(solution)/shard_map/reduce_sum | solution.py:71
  426.0 239.9 %all-gather.5.cloned.1.call-done = bf16[12288,512]{1,0:T(8,128)(2,1)} async-done(((bf16[192,512]{1,0:T(8,128)(2,1)}), bf16[12288,512]{1,0:T(8,128)(2,1)}) %all-gather.5.cloned.1.call-update) | async-done | bytes 12582928 | tf_op jit(solution)/shard_map/all_gather | solution.py:105
  666.0 16.5 %copy.13 = bf16[12288,512]{0,1:T(8,128)(2,1)} copy(bf16[12288,512]{1,0:T(8,128)(2,1)} %all-gather.5.cloned.1.call-done) | data formatting | bytes 25165824 | tf_op jit(solution)/shard_map/all_gather | solution.py:105
  682.5 21.5 %fusion.5 = bf16[192,8,64]{0,2,1:T(8,128)(2,1)} fusion(bf16[12288,8,64]{0,2,1:T(8,128)(2,1)} %bitcast.77, bf16[8,192,12288]{2,1,0:T(8,128)(2,1)} %get-tuple-element.8, f32[192,8]{0,1:T(8,128)S(1)} %bitcast.81, f32[192,8]{0,1:T(8,128)S(1)} %get-tuple-element.44), kind=kOutput, calls=%fused_computation.38 | convolution fusion | flops 2416214016 | bytes 50540544 | tf_op jit(solution)/shard_map/hqk,khd->qhd/dot_general | solution.py:72
  704.0 1.9 fusion.2
  706.5 3.2 fusion.58
  709.7 0.8 fusion.20
  710.5 4.0 collective-permute-start
  714.5 2.1 collective-permute-start.1
  716.6 1.1 fusion.55
  717.8 3.4 collective-permute-done.1
  721.2 5.5 fusion.51
  728.3 0.9 fusion.21
  (34 shorter events, 3.0 us)
Async XLA Ops:
  6.5 3.8 copy-start
  6.5 334.2 %all-gather.3.cloned.1.call-start = ((), (), s32[]{:S(2)}) async-start(), calls=%async_computation | async-start | bytes 12779520 | tf_op jit(solution)/shard_map/all_gather | solution.py:104
  13.0 653.0 %all-gather.5.cloned.1.call-start = ((), (), s32[]{:S(2)}) async-start(), calls=%async_computation.1 | async-start | bytes 12779520 | tf_op jit(solution)/shard_map/all_gather | solution.py:105
  682.5 21.5 %copy-start.2 = (bf16[1,192,1024]{2,1,0:T(8,128)(2,1)S(1)}, bf16[1,192,1024]{2,1,0:T(8,128)(2,1)}, u32[]{:S(2)}) copy-start(bf16[1,192,1024]{2,1,0:T(8,128)(2,1)} %param.7) | copy-start | bytes 1179652
  682.5 46.8 %copy-start.1 = (bf16[1024,1536]{1,0:T(8,128)(2,1)S(1)}, bf16[1024,1536]{1,0:T(8,128)(2,1)}, u32[]{:S(2)}) copy-start(bf16[1024,1536]{1,0:T(8,128)(2,1)} %param.9) | copy-start | bytes 9437188
  703.9 23.4 %copy-start.3 = (bf16[1024,1024]{1,0:T(8,128)(2,1)S(1)}, bf16[1024,1024]{1,0:T(8,128)(2,1)}, u32[]{:S(2)}) copy-start(bf16[1024,1024]{1,0:T(8,128)(2,1)} %param.13) | copy-start | bytes 6291460
  703.9 24.4 %copy-start.4 = (pred[192]{0:T(512)(128)(4,1)S(1)}, pred[192]{0:T(512)(128)(4,1)}, u32[]{:S(2)}) copy-start(pred[192]{0:T(512)(128)(4,1)} %add_compare_fusion) | copy-start | bytes 580
  710.5 7.2 collective-permute-start
  714.5 6.7 collective-permute-start.1
Sparse Core Ops, SparseCore 0:
  13.1 327.5 all-gather.2
  342.5 323.4 all-gather.4
where the time goes:
time: 737 us; the launch traced here: 736 us
  waiting for transfers between devices  567 us (77%)
  matrix products  60.1 us (8%)
  other arithmetic  51.8 us (7%)
  local copies, waits for them, and re-layouts  37 us (5%)
  between operations  14.2 us (2%)
    all_gather x1, waiting for transfers between devices, per_device(): lax.all_gather(keys, 'ctx', axis=0, tiled=True)  323 us
    all_gather x1, waiting for transfers between devices, per_device(): lax.all_gather(values, 'ctx', axis=0, tiled=True)  240 us
    reduce_sum x1, other arithmetic, attend_block(): new_sum = jnp.sum(weights, axis=-1)  37.7 us
    dot_general x1, matrix products, attend_block(): jnp.einsum('qhd,khd->hqk', query_heads, key_heads, preferred_element_type...  31 us
    dot_general x1, matrix products, attend_block(): jnp.einsum('hqk,khd->qhd', to_bf16(weights), value_heads, preferred_eleme...  21.5 us
    all_gather x1, local copies, waits for them, and re-layouts, per_device(): lax.all_gather(keys, 'ctx', axis=0, tiled=True)  16.6 us
    all_gather x1, local copies, waits for them, and re-layouts, per_device(): lax.all_gather(values, 'ctx', axis=0, tiled=True)  16.5 us
  transfers between devices with their start and end apart: 4, of which 3 were waited for; matrix products, arithmetic and copies ran while one was open for 12% of the time, Pallas kernels for 0%

commit v1 on v0

--- a/solution.py
+++ b/solution.py
@@ -101,7 +101,9 @@
     run_max, run_sum, run_acc = attend_block(
         initial,
         queries,
-        lax.all_gather(keys, "ctx", axis=0, tiled=True),
+        jnp.concatenate(
+            lax.all_to_all(jnp.stack([keys] * lax.axis_size("ctx")), "ctx", 0, 0), axis=0
+        ),
         lax.all_gather(values, "ctx", axis=0, tiled=True),
         limit,
     )

time: 737 us -> 610 us (0.83)
  waiting for transfers between devices: 567 us -> 383 us
  local copies, waits for them, and re-layouts: 37 us -> 74.3 us
  starting transfers between devices: 6.12 us -> 19.7 us
    all_to_all x0 -> x1, waiting for transfers between devices: none -> 350 us  [per_device(): lax.all_to_all(jnp.stack([keys] * lax.axis_size('ctx')), 'ctx', 0, 0)]
    all_gather x1 -> x0, waiting for transfers between devices: 323 us -> none  [per_device(): lax.all_gather(keys, 'ctx', axis=0, tiled=True)]
    all_gather x1, waiting for transfers between devices: 240 us -> 31.2 us  [per_device(): lax.all_gather(values, 'ctx', axis=0, tiled=True)]
    another operation x0 -> x2, local copies, waits for them, and re-layouts: none -> 30.9 us  [the longest x1 24.8 us: attend_block(): key_heads = key_piece.reshape(count, head_count, head_size)]
    all_to_all x0 -> x1, local copies, waits for them, and re-layouts: none -> 24.3 us  [per_device(): lax.all_to_all(jnp.stack([keys] * lax.axis_size('ctx')), 'ctx', 0, 0)]
    all_gather x1 -> x0, local copies, waits for them, and re-layouts: 16.6 us -> none  [per_device(): lax.all_gather(keys, 'ctx', axis=0, tiled=True)]
    all_to_all x0 -> x1, starting transfers between devices: none -> 13.4 us  [per_device(): lax.all_to_all(jnp.stack([keys] * lax.axis_size('ctx')), 'ctx', 0, 0)]
  transfers between devices with their start and end apart: 4 -> 4, of which waited for: 3 -> 3; matrix products, arithmetic and copies ran while one was open for 12% -> 20% of each run, Pallas kernels for 0% -> 0%
where the time goes in v1:
time: 610 us; the launch traced here: 603 us
  waiting for transfers between devices  383 us (63%)
  local copies, waits for them, and re-layouts  74.3 us (12%)
  matrix products  60 us (10%)
  other arithmetic  51.8 us (8%)
  starting transfers between devices  19.7 us (3%)
  between operations  14.2 us (2%)
    all_to_all x1, waiting for transfers between devices, per_device(): lax.all_to_all(jnp.stack([keys] * lax.axis_size('ctx')), 'ctx', 0, 0)  350 us
    reduce_sum x1, other arithmetic, attend_block(): new_sum = jnp.sum(weights, axis=-1)  37.7 us
    all_gather x1, waiting for transfers between devices, per_device(): lax.all_gather(values, 'ctx', axis=0, tiled=True)  31.2 us
    dot_general x1, matrix products, attend_block(): jnp.einsum('qhd,khd->hqk', query_heads, key_heads, preferred_element_type...  31 us
    another operation x1, local copies, waits for them, and re-layouts, attend_block(): key_heads = key_piece.reshape(count, head_count, head_size)  24.8 us
    all_to_all x1, local copies, waits for them, and re-layouts, per_device(): lax.all_to_all(jnp.stack([keys] * lax.axis_size('ctx')), 'ctx', 0, 0)  24.3 us
    dot_general x1, matrix products, attend_block(): jnp.einsum('hqk,khd->qhd', to_bf16(weights), value_heads, preferred_eleme...  21.5 us
    all_gather x1, local copies, waits for them, and re-layouts, per_device(): lax.all_gather(values, 'ctx', axis=0, tiled=True)  16.5 us
  transfers between devices with their start and end apart: 4, of which 3 were waited for; matrix products, arithmetic and copies ran while one was open for 20% of the time, Pallas kernels for 0%

profile of v1, /device:TPU:2, one launch (start us, length us, event | category | flops | bytes accessed | tf_op | source)
XLA Modules:
  0.0 603.3 jit_solution(12797067942810577139)
XLA Ops:
  6.5 1.3 convert_reduce_fusion.1
  7.8 1.2 fusion.13
  9.1 1.2 fusion.14
  10.3 1.9 fusion.56
  12.9 6.1 %stack.2 = bf16[64,192,512]{2,1,0:T(8,128)(2,1)} broadcast(bf16[192,512]{1,0:T(8,128)(2,1)S(1)} %get-tuple-element.9), dimensions={1,2} | broadcast | bytes 12779520 | tf_op jit(solution)/shard_map/stack | solution.py:105
  19.0 13.4 %all-to-all-start = ((bf16[64,192,512]{2,1,0:T(8,128)(2,1)}), bf16[64,192,512]{2,1,0:T(8,128)(2,1)}, u32[]{:S(2)}, u32[]{:S(2)}) async-start(bf16[64,192,512]{2,1,0:T(8,128)(2,1)} %stack.2), calls=%async_computation | async-start | bytes 25165824 | tf_op jit(solution)/shard_map/all_to_all | solution.py:105
  33.1 1.0 fusion.50
  36.2 350.0 %all-to-all-done = bf16[64,192,512]{2,1,0:T(8,128)(2,1)} async-done(((bf16[64,192,512]{2,1,0:T(8,128)(2,1)}), bf16[64,192,512]{2,1,0:T(8,128)(2,1)}, u32[]{:S(2)}, u32[]{:S(2)}) %all-to-all-start) | async-done | bytes 12582944 | tf_op jit(solution)/shard_map/all_to_all | solution.py:105
  386.2 24.3 %copy.15 = bf16[64,192,512]{1,0,2:T(8,128)(2,1)} copy(bf16[64,192,512]{2,1,0:T(8,128)(2,1)} %all-to-all-done) | data formatting | bytes 25165824 | tf_op jit(solution)/shard_map/all_to_all | solution.py:105
  410.5 24.8 %reshape_reshape.3 = bf16[12288,8,64]{0,2,1:T(8,128)(2,1)} reshape(bf16[64,192,512]{1,0,2:T(8,128)(2,1)} %copy.15) | data formatting | bytes 25165824 | tf_op jit(solution)/shard_map/reshape;reshape | solution.py:63
  435.3 31.0 %select_reduce_fusion = (f32[8,192]{1,0:T(8,128)S(1)}, f32[8,192,12288]{2,1,0:T(8,128)}) fusion(pred[12288]{0:T(1024)(128)(4,1)S(1)} %iota_compare_fusion, bf16[192,8,64]{0,2,1:T(8,128)(2,1)S(1)} %bitcast.79, bf16[12288,8,64]{0,2,1:T(8,128)(2,1)} %reshape_reshape.3), kind=kOutput, calls=%fused_computation.1 | convolution fusion | flops 2453666304 | bytes 88295424 | tf_op jit(solution)/shard_map/qhd,khd->hqk/dot_general | solution.py:65
  466.2 37.7 %fusion = (f32[8,192]{1,0:T(8,128)S(1)}, bf16[8,192,12288]{2,1,0:T(8,128)(2,1)}) fusion(f32[8,192,12288]{2,1,0:T(8,128)} %get-tuple-element.49, f32[8,192]{1,0:T(8,128)S(1)} %get-tuple-element.45, pred[12288]{0:T(1024)(128)(4,1)S(1)} %iota_compare_fusion), kind=kLoop, calls=%fused_computation.2 | loop fusion | flops 94370304 | bytes 113270784 | tf_op jit(solution)/shard_map/reduce_sum | solution.py:71
  503.9 31.2 %all-gather.2.cloned.1.call-done = bf16[12288,512]{1,0:T(8,128)(2,1)} async-done(((bf16[192,512]{1,0:T(8,128)(2,1)}), bf16[12288,512]{1,0:T(8,128)(2,1)}) %all-gather.2.cloned.1.call-update) | async-done | bytes 12582928 | tf_op jit(solution)/shard_map/all_gather | solution.py:107
  535.1 16.5 %copy.16 = bf16[12288,512]{0,1:T(8,128)(2,1)} copy(bf16[12288,512]{1,0:T(8,128)(2,1)} %all-gather.2.cloned.1.call-done) | data formatting | bytes 25165824 | tf_op jit(solution)/shard_map/all_gather | solution.py:107
  551.6 21.5 %fusion.5 = bf16[192,8,64]{0,2,1:T(8,128)(2,1)} fusion(bf16[12288,8,64]{0,2,1:T(8,128)(2,1)} %bitcast.78, bf16[8,192,12288]{2,1,0:T(8,128)(2,1)} %get-tuple-element.8, f32[192,8]{0,1:T(8,128)S(1)} %bitcast.81, f32[192,8]{0,1:T(8,128)S(1)} %get-tuple-element.44), kind=kOutput, calls=%fused_computation.38 | convolution fusion | flops 2416214016 | bytes 50540544 | tf_op jit(solution)/shard_map/hqk,khd->qhd/dot_general | solution.py:72
  573.1 1.9 fusion.2
  575.6 3.2 fusion.58
  578.8 0.9 fusion.20
  579.7 1.9 collective-permute-start
  581.6 4.1 collective-permute-start.1
  585.8 1.1 fusion.55
  586.9 1.4 collective-permute-done.1
  588.4 5.5 fusion.51
  595.5 0.9 fusion.21
  (37 shorter events, 5.0 us)
Async XLA Ops:
  6.5 3.8 copy-start
  19.0 16.6 %copy-start.4 = (f32[31,1024]{1,0:T(8,128)S(1)}, f32[31,1024]{1,0:T(8,128)}, u32[]{:S(2)}) copy-start(f32[31,1024]{1,0:T(8,128)} %param.12) | copy-start | bytes 380932
  19.0 367.2 %all-to-all-start = ((bf16[64,192,512]{2,1,0:T(8,128)(2,1)}), bf16[64,192,512]{2,1,0:T(8,128)(2,1)}, u32[]{:S(2)}, u32[]{:S(2)}) async-start(bf16[64,192,512]{2,1,0:T(8,128)(2,1)} %stack.2), calls=%async_computation | async-start | bytes 25165824 | tf_op jit(solution)/shard_map/all_to_all | solution.py:105
  32.4 502.7 %all-gather.2.cloned.1.call-start = ((), (), s32[]{:S(2)}) async-start(), calls=%async_computation.1 | async-start | bytes 12779520 | tf_op jit(solution)/shard_map/all_gather | solution.py:107
  551.6 21.5 %copy-start.2 = (bf16[1,192,1024]{2,1,0:T(8,128)(2,1)S(1)}, bf16[1,192,1024]{2,1,0:T(8,128)(2,1)}, u32[]{:S(2)}) copy-start(bf16[1,192,1024]{2,1,0:T(8,128)(2,1)} %param.7) | copy-start | bytes 1179652
  551.6 44.8 %copy-start.1 = (bf16[1024,1536]{1,0:T(8,128)(2,1)S(1)}, bf16[1024,1536]{1,0:T(8,128)(2,1)}, u32[]{:S(2)}) copy-start(bf16[1024,1536]{1,0:T(8,128)(2,1)} %param.9) | copy-start | bytes 9437188
  573.1 21.4 %copy-start.3 = (bf16[1024,1024]{1,0:T(8,128)(2,1)S(1)}, bf16[1024,1024]{1,0:T(8,128)(2,1)}, u32[]{:S(2)}) copy-start(bf16[1024,1024]{1,0:T(8,128)(2,1)} %param.13) | copy-start | bytes 6291460
  573.1 22.4 %copy-start.5 = (pred[192]{0:T(512)(128)(4,1)S(1)}, pred[192]{0:T(512)(128)(4,1)}, u32[]{:S(2)}) copy-start(pred[192]{0:T(512)(128)(4,1)} %add_compare_fusion) | copy-start | bytes 580
  579.7 7.2 %collective-permute-start = (bf16[15,1024]{1,0:T(8,128)(2,1)S(1)}, bf16[15,1024]{1,0:T(8,128)(2,1)S(1)}, u32[]{:S(2)}, u32[]{:S(2)}) collective-permute-start(bf16[15,1024]{1,0:T(8,128)(2,1)S(1)} %get-tuple-element.11), channel_id=1, source_target_pairs={{0,1},{1,2},{2,3},{3,4},{4,5},{5,6},{6,7},{7,8},{8,9},{9,10},{10,1... | collective-permute-start | bytes 92168 | tf_op jit(solution)/shard_map/ppermute | solution.py:19
  581.6 6.7 %collective-permute-start.1 = (bf16[15,1024]{1,0:T(8,128)(2,1)S(1)}, bf16[15,1024]{1,0:T(8,128)(2,1)S(1)}, u32[]{:S(2)}, u32[]{:S(2)}) collective-permute-start(bf16[15,1024]{1,0:T(8,128)(2,1)S(1)} %get-tuple-element.12), channel_id=1, source_target_pairs={{1,0},{2,1},{3,2},{4,3},{5,4},{6,5},{7,6},{8,7},{9,8},{10,9},{11,1... | collective-permute-start | bytes 92168 | tf_op jit(solution)/shard_map/ppermute | solution.py:21
Sparse Core Ops, SparseCore 0:
  35.0 500.0 all-gather.1
